TPU v7x, 256 devices: a whole 4x4x8 slice. The times are simulated.
256 devices in a mesh: pix: 64 (over x, z, core), band: 4 (over y).
Axes of the slice: x: 4, y: 4, z: 8, core: 2. Of those that a mesh axis runs over, the one named last changes fastest.
Arguments:
- spectra: bfloat16 [224, 262144], P('band', 'pix'), may hold values from -0.1 to 4
- endmembers: bfloat16 [224, 512], P('band'), may hold values from 0.05 to 1
- gram_inverse: float32 [512, 512], replicated, may hold values from -1 to 1, as said below
- abundances: float32 [512, 262144], P(None, ('pix', 'band')), may hold values from 0 to 512, as said below
- duals: float32 [512, 262144], P(None, ('pix', 'band')), may hold values from -4 to 4
Outputs:
- abundances_out: float32 [512, 262144], P(None, ('pix', 'band'))
- duals_out: float32 [512, 262144], P(None, ('pix', 'band'))
- residual_rms: float32 [2, 2], replicated
Inputs may be any that keep to these rules, and one draw needn't show every extreme that they name: `abundances`: each column is nonnegative and sums to 512. `gram_inverse`: penalty times the float32 inverse of endmembers^T endmembers / 512^2 + penalty I, with penalty = 224 / (2 * 512^2) and the endmembers as stored.
All inputs are finite; a program needn't handle non-finite values.
Results may differ from a plain program's by a relative error of at most 0.0004.
Values may be sent and summed in bfloat16 or wider, within the bound.
A program may use at most 64 MiB of HBM per device.

v0:
```python
import jax
import jax.numpy as jnp
from jax import lax
from jax.sharding import Mesh
from jax.sharding import PartitionSpec as P

B = 224
K = 512
ITERS = 2
BISECT = 6
PIX = ("pix_0", "pix_1", "pix_2")
PIX_BAND = ("pix_0", "pix_1", "pix_2", "band")


def one_axis_at_a_time(shard, axes):
    for axis in axes:
        shard = lax.psum(shard, axis)
    return shard


def project(shifted):
    simplex_sum = float(K)
    high_end = jnp.max(shifted, axis=0)
    low_end = (jnp.sum(shifted, axis=0) - simplex_sum) / simplex_sum

    def mass_at(level):
        return jnp.sum(jnp.maximum(shifted - level[None, :], 0.0), axis=0)

    mass_low = mass_at(low_end)
    mass_high = jnp.zeros_like(high_end)

    def bisect_once(unused, state):
        low_now, high_now, low_mass, high_mass = state
        middle = 0.5 * (low_now + high_now)
        total_mass = mass_at(middle)
        too_high = total_mass > simplex_sum
        return (
            jnp.where(too_high, middle, low_now),
            jnp.where(too_high, high_now, middle),
            jnp.where(too_high, total_mass, low_mass),
            jnp.where(too_high, high_mass, total_mass),
        )

    low_end, high_end, mass_low, mass_high = lax.fori_loop(
        0, BISECT, bisect_once, (low_end, high_end, mass_low, mass_high)
    )
    level = low_end + (mass_low - simplex_sum) * (high_end - low_end) / (mass_low - mass_high)
    return jnp.maximum(shifted - level[None, :], 0.0)


def contract_bands(signatures, columns):
    return lax.dot_general(
        signatures, columns, (((0,), (0,)), ((), ())), preferred_element_type=jnp.float32
    )


def body(spectra, endmembers, gram_inverse, abundances, duals):
    penalty = B / (2.0 * K * K)
    exchanged = lax.all_to_all(spectra, "band", split_axis=1, concat_axis=0, tiled=True)
    all_rows = lax.all_gather(endmembers, "band", axis=0, tiled=True)
    fit_term = contract_bands(all_rows, exchanged)
    fit_term = fit_term / K
    pixel_count = abundances.shape[1] * lax.axis_size(PIX) * lax.axis_size("band")
    current = abundances
    scaled_dual = duals
    primal_list = []
    change_list = []
    for sweep in range(ITERS):
        primal = jnp.dot(
            gram_inverse,
            fit_term / penalty + current - scaled_dual,
            precision=lax.Precision.HIGHEST,
        )
        updated = project(primal + scaled_dual)
        scaled_dual = scaled_dual + primal - updated
        primal_sum = jnp.sum((primal - updated) ** 2)
        change_sum = jnp.sum((updated - current) ** 2)
        primal_list.append(primal_sum)
        change_list.append(change_sum)
        current = updated
    totals = jnp.stack([jnp.stack(primal_list), jnp.stack(change_list)])
    totals = one_axis_at_a_time(totals, PIX_BAND)
    residual_rms = jnp.sqrt(totals / pixel_count)
    return (current, scaled_dual, residual_rms)


def solution(mesh):
    finer = Mesh(
        mesh.devices.reshape(4, 8, 2, mesh.shape["band"]), ("pix_0", "pix_1", "pix_2", "band")
    )
    return jax.shard_map(
        body,
        mesh=finer,
        in_specs=(P("band", PIX), P("band", None), P(), P(None, PIX_BAND), P(None, PIX_BAND)),
        out_specs=(P(None, PIX_BAND), P(None, PIX_BAND), P()),
        check_vma=False,
    )
```

profile of v0, /device:TPU:1, one launch (start us, length us, event | category | flops | bytes accessed | tf_op | source)
XLA Modules:
  0.0 109.2 jit_solution(441457199507730125)
XLA Ops:
  0.6 0.0 copy-start
  0.6 1.9 %copy.12 = bf16[7,4,8,1024]{3,2,0,1:T(8,128)(2,1)} copy(bf16[7,4,8,1024]{3,2,1,0:T(8,128)(2,1)} %bitcast.36) | data formatting | bytes 917504 | tf_op jit(solution)/shard_map/all_to_all | solution.py:59
  2.5 5.0 %all-to-all-start = ((bf16[56,4,1024]{2,0,1:T(8,128)(2,1)}), bf16[56,4,1024]{2,0,1:T(8,128)(2,1)S(1)}, u32[]{:S(2)}, u32[]{:S(2)}) async-start(bf16[56,4,1024]{2,0,1:T(8,128)(2,1)} %bitcast.34), calls=%async_computation | async-start | bytes 917504 | tf_op jit(solution)/shard_map/all_to_all | solution.py:59
  7.6 12.5 %all_gather.3 = bf16[224,512]{1,0:T(8,128)(2,1)S(1)} all-gather(bf16[56,512]{1,0:T(8,128)(2,1)} %param.10), channel_id=1, replica_groups=mesh['pix_0'=4,'pix_1'=8,'pix_2'=2,'band'=4] {'band'}, dimensions={0}, use_global_device_ids=true | all-gather | bytes 286720 | tf_op jit(solution)/shard_map/all_gather | solution.py:60
  20.0 0.5 fusion.29
  20.5 8.7 %fusion.28 = (f32[1024]{0:T(1024)S(1)}, f32[512,1024]{1,0:T(8,128)S(1)}, f32[1024,512]{0,1:T(8,128)}) fusion(f32[512,1024]{1,0:T(8,128)} %param.13, f32[512,512]{1,0:T(8,128)S(1)} %copy-done, f32[512,1024]{1,0:T(8,128)} %param.12, f32[512,1024]{1,0:T(8,128)S(1)} %fusion.29), kind=kOutput, calls=%fused_computation.54 | convolution fusion | flops 3223845888 | bytes 11538432 | tf_op jit(solution)/shard_map/dot_general | solution.py:69
  29.2 0.3 maximum_reduce_fusion.3
  29.5 1.9 %while.34 = (s32[]{:T(128)}, f32[1024]{0:T(1024)S(1)}, f32[1024]{0:T(1024)S(1)}, f32[1024]{0:T(1024)S(1)}, f32[1024]{0:T(1024)S(1)}, /*index=5*/f32[512,1024]{1,0:T(8,128)S(1)}, s32[]{:T(128)}, s32[]{:T(128)}) while((s32[]{:T(128)}, f32[1024]{0:T(1024)S(1)}, f32[1024]{0:T(1024)S(1)}, f32[1024]{0:T(1024)S(1)}, f32[1024]{0:T(1024)S(1)}, ...), condition=%wide.region_5.6_spmd.clone, body=%wide.region_3.5_spmd.clone.sunk | while | flops 1582083 | bytes 2154591 | solution.py:44
  29.6 0.3 maximum_reduce_fusion.6
  29.9 0.3 maximum_reduce_fusion.6
  30.2 0.3 maximum_reduce_fusion.6
  30.5 0.3 maximum_reduce_fusion.6
  30.8 0.3 maximum_reduce_fusion.6
  31.2 0.3 maximum_reduce_fusion.6
  31.5 7.0 %fusion.27 = (f32[1024]{0:T(1024)S(1)}, f32[512,1024]{1,0:T(8,128)S(1)}, f32[1024,512]{0,1:T(8,128)}) fusion(f32[512,1024]{1,0:T(8,128)S(1)} %get-tuple-element.310, f32[1024]{0:T(1024)S(1)} %divide_add_fusion.1, f32[512,512]{1,0:T(8,128)S(1)} %copy-done, f32[512,1024]{1,0:T(8,128)} %copy-done.2), kind=kOutput, calls=%fused_computation.53 | convolution fusion | flops 3226991616 | bytes 9445376 | tf_op jit(solution)/shard_map/dot_general | solution.py:69
  38.5 0.3 maximum_reduce_fusion.2
  38.8 1.0 copy-done.1
  39.8 11.3 %while.35 = (s32[]{:T(128)}, f32[1024]{0:T(1024)S(1)}, f32[1024]{0:T(1024)S(1)}, f32[1024]{0:T(1024)S(1)}, f32[1024]{0:T(1024)S(1)}, /*index=5*/f32[512,1024]{1,0:T(8,128)}, s32[]{:T(128)}, s32[]{:T(128)}) while((s32[]{:T(128)}, f32[1024]{0:T(1024)S(1)}, f32[1024]{0:T(1024)S(1)}, f32[1024]{0:T(1024)S(1)}, f32[1024]{0:T(1024)S(1)}, ...), condition=%wide.region_11.12_spmd.clone, body=%wide.region_9.0_spmd.clone.sunk | while | flops 1582083 | bytes 2154591 | solution.py:44
  39.8 1.8 %maximum_reduce_fusion.7 = f32[1024]{0:T(1024)S(1)} fusion(f32[512,1024]{1,0:T(8,128)} %get-tuple-element.307, f32[1024]{0:T(1024)S(1)} %add_multiply_fusion.7), kind=kLoop, calls=%fused_computation.7.clone.1 | loop fusion | flops 1571840 | bytes 2105344 | tf_op jit(solution)/shard_map/while/body/eval_jaxpr/reduce_sum | solution.py:27
  41.7 1.8 %maximum_reduce_fusion.7 = f32[1024]{0:T(1024)S(1)} fusion(f32[512,1024]{1,0:T(8,128)} %get-tuple-element.307, f32[1024]{0:T(1024)S(1)} %add_multiply_fusion.7), kind=kLoop, calls=%fused_computation.7.clone.1 | loop fusion | flops 1571840 | bytes 2105344 | tf_op jit(solution)/shard_map/while/body/eval_jaxpr/reduce_sum | solution.py:27
  43.6 1.8 %maximum_reduce_fusion.7 = f32[1024]{0:T(1024)S(1)} fusion(f32[512,1024]{1,0:T(8,128)} %get-tuple-element.307, f32[1024]{0:T(1024)S(1)} %add_multiply_fusion.7), kind=kLoop, calls=%fused_computation.7.clone.1 | loop fusion | flops 1571840 | bytes 2105344 | tf_op jit(solution)/shard_map/while/body/eval_jaxpr/reduce_sum | solution.py:27
  45.5 1.8 %maximum_reduce_fusion.7 = f32[1024]{0:T(1024)S(1)} fusion(f32[512,1024]{1,0:T(8,128)} %get-tuple-element.307, f32[1024]{0:T(1024)S(1)} %add_multiply_fusion.7), kind=kLoop, calls=%fused_computation.7.clone.1 | loop fusion | flops 1571840 | bytes 2105344 | tf_op jit(solution)/shard_map/while/body/eval_jaxpr/reduce_sum | solution.py:27
  47.3 1.8 %maximum_reduce_fusion.7 = f32[1024]{0:T(1024)S(1)} fusion(f32[512,1024]{1,0:T(8,128)} %get-tuple-element.307, f32[1024]{0:T(1024)S(1)} %add_multiply_fusion.7), kind=kLoop, calls=%fused_computation.7.clone.1 | loop fusion | flops 1571840 | bytes 2105344 | tf_op jit(solution)/shard_map/while/body/eval_jaxpr/reduce_sum | solution.py:27
  49.2 1.8 %maximum_reduce_fusion.7 = f32[1024]{0:T(1024)S(1)} fusion(f32[512,1024]{1,0:T(8,128)} %get-tuple-element.307, f32[1024]{0:T(1024)S(1)} %add_multiply_fusion.7), kind=kLoop, calls=%fused_computation.7.clone.1 | loop fusion | flops 1571840 | bytes 2105344 | tf_op jit(solution)/shard_map/while/body/eval_jaxpr/reduce_sum | solution.py:27
  51.1 7.0 %fusion.9 = (f32[]{:T(128)}, f32[]{:T(128)}, f32[]{:T(128)}, f32[]{:T(128)}, f32[512,1024]{1,0:T(8,128)}) fusion(f32[1024,512]{0,1:T(8,128)} %get-tuple-element.168, f32[512,1024]{1,0:T(8,128)S(1)} %get-tuple-element.310, f32[1024]{0:T(1024)S(1)} %divide_add_fusion.1, f32[512,1024]{1,0:T(8,128)} %param.12, f32[1024,512]{0,1:T(8,128)} %get-tuple-element.169, ...), kind=kLoop, calls=%fused_computation.21 | loop fusion | flops 8388604 | bytes 12591120 | tf_op jit(solution)/shard_map/reduce_sum | solution.py:76
  58.1 2.6 %maximum_bitcast_fusion = (f32[1,2]{1,0:T(1,128)S(1)}, f32[1,2]{1,0:T(1,128)S(1)}) fusion(f32[1]{0:T(128)} %bitcast.5, f32[1]{0:T(128)} %bitcast.4, f32[1]{0:T(128)} %bitcast.8, f32[1]{0:T(128)} %bitcast.7), kind=kLoop, calls=%fused_computation.48 | loop fusion | flops 4 | bytes 32 | tf_op jit(solution)/shard_map/stack | solution.py:81
  60.7 8.0 %psum.28 = f32[2,2]{1,0:T(2,128)S(1)} all-reduce(f32[2,2]{1,0:T(2,128)S(1)} %pad_maximum_fusion), channel_id=1, replica_groups=mesh['pix_0'=4,'pix_1'=8,'pix_2'=2,'band'=4] {'pix_0'}, use_global_device_ids=true, to_apply=%region_16.17 | all-reduce | flops 4 | bytes 32 | tf_op jit(solution)/shard_map/psum | solution.py:17
  68.8 16.2 %psum.29 = f32[2,2]{1,0:T(2,128)S(1)} all-reduce(f32[2,2]{1,0:T(2,128)S(1)} %psum.28), channel_id=1, replica_groups=mesh['pix_0'=4,'pix_1'=8,'pix_2'=2,'band'=4] {'pix_1'}, use_global_device_ids=true, to_apply=%region_17.18 | all-reduce | flops 4 | bytes 32 | tf_op jit(solution)/shard_map/psum | solution.py:17
  85.0 12.4 %psum.30 = f32[2,2]{1,0:T(2,128)S(1)} all-reduce(f32[2,2]{1,0:T(2,128)S(1)} %psum.29), channel_id=1, replica_groups=mesh['pix_0'=4,'pix_1'=8,'pix_2'=2,'band'=4] {'pix_2'}, use_global_device_ids=true, to_apply=%region_18.19 | all-reduce | flops 4 | bytes 32 | tf_op jit(solution)/shard_map/psum | solution.py:17
  97.4 7.1 %psum.31 = f32[2,2]{1,0:T(2,128)S(1)} all-reduce(f32[2,2]{1,0:T(2,128)S(1)} %psum.30), channel_id=1, replica_groups=mesh['pix_0'=4,'pix_1'=8,'pix_2'=2,'band'=4] {'band'}, use_global_device_ids=true, to_apply=%region_19.20 | all-reduce | flops 4 | bytes 32 | tf_op jit(solution)/shard_map/psum | solution.py:17
  104.5 0.6 multiply_sqrt_fusion
  105.1 4.1 %sub.115 = f32[512,1024]{1,0:T(8,128)} subtract(f32[512,1024]{1,0:T(8,128)} %get-tuple-element.311, f32[512,1024]{1,0:T(8,128)} %get-tuple-element.155) | non-fusion elementwise | flops 524288 | bytes 6291456 | tf_op jit(solution)/shard_map/sub | solution.py:75
  (36 shorter events, 0.2 us)
Async XLA Ops:
  0.6 19.9 %copy-start = (f32[512,512]{1,0:T(8,128)S(1)}, f32[512,512]{1,0:T(8,128)}, u32[]{:S(2)}) copy-start(f32[512,512]{1,0:T(8,128)} %param.11) | copy-start | bytes 3145732
  2.5 17.5 %all-to-all-start = ((bf16[56,4,1024]{2,0,1:T(8,128)(2,1)}), bf16[56,4,1024]{2,0,1:T(8,128)(2,1)S(1)}, u32[]{:S(2)}, u32[]{:S(2)}) async-start(bf16[56,4,1024]{2,0,1:T(8,128)(2,1)} %bitcast.34), calls=%async_computation | async-start | bytes 917504 | tf_op jit(solution)/shard_map/all_to_all | solution.py:59
  20.5 8.7 %copy-start.2 = (f32[512,1024]{1,0:T(8,128)}, f32[512,1024]{1,0:T(8,128)S(1)}, u32[]{:S(2)}) copy-start(f32[512,1024]{1,0:T(8,128)S(1)} %fusion.29) | copy-start | bytes 6291460
  38.5 1.4 %copy-start.1 = (f32[512,1024]{1,0:T(8,128)}, f32[512,1024]{1,0:T(8,128)S(1)}, u32[]{:S(2)}) copy-start(f32[512,1024]{1,0:T(8,128)S(1)} %get-tuple-element.291) | copy-start | bytes 6291460
where the time goes:
time: 110 us; the launch traced here: 109 us
  blocking collectives  56.2 us (51%)
  other arithmetic  27.9 us (25%)
  matrix products  16.1 us (15%)
  starting transfers between devices  5 us (5%)
  local copies, waits for them, and re-layouts  2.93 us (3%)
    psum x4, blocking collectives, one_axis_at_a_time(): shard = lax.psum(shard, axis)  43.7 us
    dot_general x2, matrix products, body(): jnp.dot(gram_inverse, fit_term / penalty + current - scaled_dual, precisi...  15.7 us
    reduce_sum x14, other arithmetic, mass_at(): return jnp.sum(jnp.maximum(shifted - level[None, :], 0.0), axis=0)  13.3 us
    all_gather x1, blocking collectives, body(): all_rows = lax.all_gather(endmembers, 'band', axis=0, tiled=True)  12.5 us
    reduce_sum x1, other arithmetic, body(): primal_sum = jnp.sum((primal - updated) ** 2)  7.01 us
    all_to_all x1, starting transfers between devices, body(): lax.all_to_all(spectra, 'band', split_axis=1, concat_axis=0, tiled=True)  5 us
    sub x1, other arithmetic, body(): scaled_dual = scaled_dual + primal - updated  4.1 us
    another operation x2, other arithmetic, body(): totals = jnp.stack([jnp.stack(primal_list), jnp.stack(change_list)])  2.64 us
  transfers between devices with their start and end apart: 1, of which 0 were waited for; matrix products, arithmetic and copies ran while one was open for 0% of the time, Pallas kernels for 0%

commit v1 on v0

--- a/solution.py
+++ b/solution.py
@@ -10,6 +10,18 @@
 BISECT = 6
 PIX = ("pix_0", "pix_1", "pix_2")
 PIX_BAND = ("pix_0", "pix_1", "pix_2", "band")
+
+
+def in_blocks(x, dim, size):
+    dims = x.shape
+    blocks = x.reshape(*dims[:dim], size, dims[dim] // size, *dims[dim + 1 :])
+    return jnp.moveaxis(blocks, dim, 0)
+
+
+def joined_along(blocks, dim):
+    blocks = jnp.moveaxis(blocks, 0, dim)
+    lengths = blocks.shape
+    return blocks.reshape(*lengths[:dim], lengths[dim] * lengths[dim + 1], *lengths[dim + 2 :])
 
 
 def one_axis_at_a_time(shard, axes):
@@ -56,7 +68,14 @@
 
 def body(spectra, endmembers, gram_inverse, abundances, duals):
     penalty = B / (2.0 * K * K)
-    exchanged = lax.all_to_all(spectra, "band", split_axis=1, concat_axis=0, tiled=True)
+    count, index = (lax.axis_size("band"), lax.axis_index("band"))
+    blocks = in_blocks(spectra, 1, count)
+    outs = [blocks[index]]
+    for step in range(1, count):
+        sent = blocks[index ^ step]
+        outs.append(lax.ppermute(sent, "band", [(i, i ^ step) for i in range(count)]))
+    blocks = jnp.stack(outs)[index ^ jnp.arange(count)]
+    exchanged = joined_along(blocks, 0)
     all_rows = lax.all_gather(endmembers, "band", axis=0, tiled=True)
     fit_term = contract_bands(all_rows, exchanged)
     fit_term = fit_term / K

time: 110 us -> 118 us (1.073)
  local copies, waits for them, and re-layouts: 2.93 us -> 21 us
  other arithmetic: 27.9 us -> 19.3 us
    unnamed x6 -> x20, local copies, waits for them, and re-layouts: 1.02 us -> 16.3 us
    reduce_sum x14, other arithmetic: 13.3 us -> 7.65 us  [mass_at(): return jnp.sum(jnp.maximum(shifted - level[None, :], 0.0), axis=0)]
    all_to_all x1 -> x0, starting transfers between devices: 5 us -> none  [body(): lax.all_to_all(spectra, 'band', split_axis=1, concat_axis=0, tiled=True)]
    ppermute x0 -> x3, starting transfers between devices: none -> 4.74 us  [body(): lax.ppermute(sent, 'band', [(i, i ^ step) for i in range(count)])]
    sub x1 -> x0, other arithmetic: 4.1 us -> none  [body(): scaled_dual = scaled_dual + primal - updated]
    gather x0 -> x1, local copies, waits for them, and re-layouts: none -> 2.36 us  [body(): blocks = jnp.stack(outs)[index ^ jnp.arange(count)]]
    all_to_all x1 -> x0, local copies, waits for them, and re-layouts: 1.9 us -> none  [body(): lax.all_to_all(spectra, 'band', split_axis=1, concat_axis=0, tiled=True)]
    another operation x0 -> x1, other arithmetic: none -> 1.84 us  [body(): blocks = jnp.stack(outs)[index ^ jnp.arange(count)]]
  transfers between devices with their start and end apart: 1 -> 3, of which waited for: 0 -> 0; matrix products, arithmetic and copies ran while one was open for 0% -> 6% of each run, Pallas kernels for 0% -> 0%
where the time goes in v1:
time: 118 us; the launch traced here: 117 us
  blocking collectives  55.1 us (47%)
  local copies, waits for them, and re-layouts  21 us (18%)
  other arithmetic  19.3 us (16%)
  matrix products  15.7 us (13%)
  starting transfers between devices  4.74 us (4%)
    psum x4, blocking collectives, one_axis_at_a_time(): shard = lax.psum(shard, axis)  43 us
    unnamed x20, local copies, waits for them, and re-layouts  16.3 us
    dot_general x2, matrix products, body(): jnp.dot(gram_inverse, fit_term / penalty + current - scaled_dual, precisi...  14.1 us
    all_gather x1, blocking collectives, body(): all_rows = lax.all_gather(endmembers, 'band', axis=0, tiled=True)  12.1 us
    reduce_sum x14, other arithmetic, mass_at(): return jnp.sum(jnp.maximum(shifted - level[None, :], 0.0), axis=0)  7.65 us
    reduce_sum x1, other arithmetic, body(): primal_sum = jnp.sum((primal - updated) ** 2)  6.42 us
    ppermute x3, starting transfers between devices, body(): lax.ppermute(sent, 'band', [(i, i ^ step) for i in range(count)])  4.74 us
    another operation x2, other arithmetic, body(): totals = jnp.stack([jnp.stack(primal_list), jnp.stack(change_list)])  2.57 us
  transfers between devices with their start and end apart: 3, of which 0 were waited for; matrix products, arithmetic and copies ran while one was open for 6% of the time, Pallas kernels for 0%

profile of v1, /device:TPU:1, one launch (start us, length us, event | category | flops | bytes accessed | tf_op | source)
XLA Modules:
  0.0 117.0 jit_solution(10070453341550499028)
XLA Ops:
  0.7 1.4 %reshape.47 = bf16[56,4,1024]{2,1,0:T(4,128)(2,1)S(1)} reshape(bf16[56,4096]{1,0:T(8,128)(2,1)} %param.9) | data formatting | bytes 917504 | tf_op jit(solution)/shard_map/reshape | solution.py:17
  2.1 1.0 constant_dynamic-slice_fusion.3
  3.1 0.7 copy.50
  3.8 2.1 %collective-permute-start = (bf16[56,1024]{1,0:T(8,128)(2,1)}, bf16[56,1024]{1,0:T(8,128)(2,1)}, u32[]{:S(2)}, u32[]{:S(2)}) collective-permute-start(bf16[56,1024]{1,0:T(8,128)(2,1)} %bitcast.57), channel_id=1, source_target_pairs={{0,1},{1,0},{2,3},{3,2},{4,5},{5,4},{6,7},{7,6},{8,9},{9,8},{10,11... | collective-permute-start | bytes 344072 | tf_op jit(solution)/shard_map/ppermute | solution.py:76
  5.9 0.7 copy.49
  6.6 2.6 %collective-permute-start.1 = (bf16[56,1024]{1,0:T(8,128)(2,1)}, bf16[56,1024]{1,0:T(8,128)(2,1)}, u32[]{:S(2)}, u32[]{:S(2)}) collective-permute-start(bf16[56,1024]{1,0:T(8,128)(2,1)} %bitcast.56), channel_id=1, source_target_pairs={{0,2},{1,3},{2,0},{3,1},{4,6},{5,7},{6,4},{7,5},{8,10},{9,11},{10,... | collective-permute-start | bytes 344072 | tf_op jit(solution)/shard_map/ppermute | solution.py:76
  9.2 0.7 copy.48
  9.9 12.1 %all_gather.3 = bf16[224,512]{1,0:T(8,128)(2,1)S(1)} all-gather(bf16[56,512]{1,0:T(8,128)(2,1)S(1)} %copy-done.4), channel_id=1, replica_groups=mesh['pix_0'=4,'pix_1'=8,'pix_2'=2,'band'=4] {'band'}, dimensions={0}, use_global_device_ids=true | all-gather | bytes 286720 | tf_op jit(solution)/shard_map/all_gather | solution.py:79
  22.0 1.9 %copy.28 = f32[512,1024]{0,1:T(8,128)S(1)} copy(f32[512,1024]{1,0:T(8,128)} %param.12) | data formatting | bytes 4194304 | tf_op args[3]
  23.9 3.6 %copy.29 = f32[512,1024]{0,1:T(8,128)} copy(f32[512,1024]{1,0:T(8,128)} %param.13) | data formatting | bytes 4194304 | tf_op args[4]
  27.6 1.8 %pad_maximum_fusion = bf16[4,56,1024]{2,1,0:T(8,128)(2,1)} fusion(bf16[1,56,1024]{2,1,0:T(8,128)(2,1)} %bitcast.2, bf16[1,56,1024]{2,1,0:T(8,128)(2,1)} %bitcast.1, bf16[1,56,1024]{2,1,0:T(8,128)(2,1)} %bitcast, bf16[1,56,1024]{2,1,0:T(8,128)(2,1)S(1)} %bitcast.60), kind=kLoop, calls=%fused_computation.42 | loop fusion | flops 688128 | bytes 917504 | tf_op jit(solution)/shard_map/stack | solution.py:77
  29.5 2.4 %gather_fusion = bf16[4,56,1024]{2,1,0:T(8,128)(2,1)} fusion(bf16[4,56,1024]{2,1,0:T(8,128)(2,1)} %pad_maximum_fusion, s32[1024]{0:T(1024)S(1)} %pad_clamp_fusion), kind=kCustom, calls=%fused_computation | custom fusion | bytes 917520 | tf_op jit(solution)/shard_map/gather | solution.py:77
  31.8 1.6 %fusion.31 = f32[1024,512]{1,0:T(8,128)S(1)} fusion(bf16[224,1024]{1,0:T(8,128)(2,1)} %bitcast.59, bf16[224,512]{1,0:T(8,128)(2,1)S(1)} %all_gather.3), kind=kOutput, calls=%fused_computation.68 | convolution fusion | flops 234881024 | bytes 2785280 | tf_op jit(solution)/shard_map/dot_general | solution.py:64
  33.6 5.2 %fusion.30 = (f32[1024]{0:T(1024)S(1)}, f32[512,1024]{0,1:T(8,128)}, f32[1024,512]{1,0:T(8,128)}) fusion(f32[512,1024]{0,1:T(8,128)S(1)} %copy-done.3, f32[512,512]{1,0:T(8,128)S(1)} %copy-done, f32[512,1024]{0,1:T(8,128)S(1)} %copy.28, f32[1024,512]{1,0:T(8,128)S(1)} %fusion.31), kind=kOutput, calls=%fused_computation.67 | convolution fusion | flops 3223845888 | bytes 11538432 | tf_op jit(solution)/shard_map/dot_general | solution.py:88
  38.8 1.9 %copy.32 = f32[512,1024]{1,0:T(8,128)S(1)} copy(f32[512,1024]{0,1:T(8,128)} %get-tuple-element.203) | data formatting | bytes 4194304
  40.7 2.2 %maximum_reduce_fusion.3 = (f32[1024]{0:T(1024)S(1)}, f32[1024]{0:T(1024)S(1)}) fusion(f32[512,1024]{0,1:T(8,128)} %get-tuple-element.203, f32[1024]{0:T(1024)S(1)} %add_multiply_fusion.3), kind=kLoop, calls=%fused_computation.35 | loop fusion | flops 2095104 | bytes 2109440 | tf_op jit(solution)/shard_map/reduce_sum | solution.py:39
  42.9 1.9 %while.34 = (s32[]{:T(128)}, f32[1024]{0:T(1024)S(1)}, f32[1024]{0:T(1024)S(1)}, f32[1024]{0:T(1024)S(1)}, f32[1024]{0:T(1024)S(1)}, /*index=5*/f32[512,1024]{1,0:T(8,128)S(1)}, s32[]{:T(128)}, s32[]{:T(128)}) while((s32[]{:T(128)}, f32[1024]{0:T(1024)S(1)}, f32[1024]{0:T(1024)S(1)}, f32[1024]{0:T(1024)S(1)}, f32[1024]{0:T(1024)S(1)}, ...), condition=%wide.region_5.6_spmd.clone, body=%wide.region_3.5_spmd.clone.sunk | while | flops 1582083 | bytes 2154591 | solution.py:56
  44.2 0.3 maximum_reduce_fusion.6
  44.8 8.9 %fusion.29 = (f32[1024]{0:T(1024)S(1)}, f32[512,1024]{0,1:T(8,128)}, f32[1024,512]{1,0:T(8,128)}) fusion(f32[512,1024]{0,1:T(8,128)} %get-tuple-element.203, f32[1024]{0:T(1024)S(1)} %divide_add_fusion.1, f32[512,512]{1,0:T(8,128)S(1)} %copy-done, f32[1024,512]{1,0:T(8,128)} %copy-done.2), kind=kOutput, calls=%fused_computation.66 | convolution fusion | flops 3226991616 | bytes 9445376 | tf_op jit(solution)/shard_map/dot_general | solution.py:88
  53.7 1.9 %copy.34 = f32[512,1024]{1,0:T(8,128)S(1)} copy(f32[512,1024]{0,1:T(8,128)} %get-tuple-element.201) | data formatting | bytes 4194304
  55.6 2.2 %maximum_reduce_fusion.2 = (f32[1024]{0:T(1024)S(1)}, f32[1024]{0:T(1024)S(1)}) fusion(f32[512,1024]{0,1:T(8,128)} %get-tuple-element.201, f32[1024]{0:T(1024)S(1)} %add_multiply_fusion.2), kind=kLoop, calls=%fused_computation.32 | loop fusion | flops 2095104 | bytes 2109440 | tf_op jit(solution)/shard_map/reduce_sum | solution.py:39
  57.8 1.9 %while.35 = (s32[]{:T(128)}, f32[1024]{0:T(1024)S(1)}, f32[1024]{0:T(1024)S(1)}, f32[1024]{0:T(1024)S(1)}, f32[1024]{0:T(1024)S(1)}, /*index=5*/f32[512,1024]{1,0:T(8,128)S(1)}, s32[]{:T(128)}, s32[]{:T(128)}) while((s32[]{:T(128)}, f32[1024]{0:T(1024)S(1)}, f32[1024]{0:T(1024)S(1)}, f32[1024]{0:T(1024)S(1)}, ...), condition=%wide.region_11.12_spmd.clone, body=%wide.region_9.0_spmd.clone.sunk | while | flops 1582083 | bytes 2154591 | solution.py:56
  58.8 0.3 maximum_reduce_fusion.7
  59.7 6.4 %fusion.9 = (f32[]{:T(128)}, f32[]{:T(128)}, f32[]{:T(128)}, f32[]{:T(128)}, f32[512,1024]{0,1:T(8,128)}, /*index=5*/f32[512,1024]{0,1:T(8,128)S(1)}) fusion(f32[1024,512]{1,0:T(8,128)} %get-tuple-element.218, f32[512,1024]{0,1:T(8,128)} %get-tuple-element.203, f32[1024]{0:T(1024)S(1)} %divide_add_fusion.1, f32[512,1024]{0,1:T(8,128)} %copy-done.1, ...), kind=kLoop, calls=%fused_computation.22 | loop fusion | flops 8912892 | bytes 14688272 | tf_op jit(solution)/shard_map/reduce_sum | solution.py:95
  66.1 2.6 %maximum_bitcast_fusion = (f32[1,2]{1,0:T(1,128)S(1)}, f32[1,2]{1,0:T(1,128)S(1)}) fusion(f32[1]{0:T(128)} %bitcast.9, f32[1]{0:T(128)} %bitcast.8, f32[1]{0:T(128)} %bitcast.12, f32[1]{0:T(128)} %bitcast.11), kind=kLoop, calls=%fused_computation.60 | loop fusion | flops 4 | bytes 32 | tf_op jit(solution)/shard_map/stack | solution.py:100
  68.7 8.5 %psum.28 = f32[2,2]{1,0:T(2,128)S(1)} all-reduce(f32[2,2]{1,0:T(2,128)S(1)} %pad_maximum_fusion.1), channel_id=1, replica_groups=mesh['pix_0'=4,'pix_1'=8,'pix_2'=2,'band'=4] {'pix_0'}, use_global_device_ids=true, to_apply=%region_16.17 | all-reduce | flops 4 | bytes 32 | tf_op jit(solution)/shard_map/psum | solution.py:29
  77.2 16.2 %psum.29 = f32[2,2]{1,0:T(2,128)S(1)} all-reduce(f32[2,2]{1,0:T(2,128)S(1)} %psum.28), channel_id=1, replica_groups=mesh['pix_0'=4,'pix_1'=8,'pix_2'=2,'band'=4] {'pix_1'}, use_global_device_ids=true, to_apply=%region_17.18 | all-reduce | flops 4 | bytes 32 | tf_op jit(solution)/shard_map/psum | solution.py:29
  93.4 10.8 %psum.30 = f32[2,2]{1,0:T(2,128)S(1)} all-reduce(f32[2,2]{1,0:T(2,128)S(1)} %psum.29), channel_id=1, replica_groups=mesh['pix_0'=4,'pix_1'=8,'pix_2'=2,'band'=4] {'pix_2'}, use_global_device_ids=true, to_apply=%region_18.19 | all-reduce | flops 4 | bytes 32 | tf_op jit(solution)/shard_map/psum | solution.py:29
  104.2 2.9 %copy.36 = f32[512,1024]{1,0:T(8,128)} copy(f32[512,1024]{0,1:T(8,128)} %get-tuple-element.212) | data formatting | bytes 4194304
  107.1 7.6 %psum.31 = f32[2,2]{1,0:T(2,128)S(1)} all-reduce(f32[2,2]{1,0:T(2,128)S(1)} %psum.30), channel_id=1, replica_groups=mesh['pix_0'=4,'pix_1'=8,'pix_2'=2,'band'=4] {'band'}, use_global_device_ids=true, to_apply=%region_19.20 | all-reduce | flops 4 | bytes 32 | tf_op jit(solution)/shard_map/psum | solution.py:29
  114.6 0.6 multiply_sqrt_fusion
  115.2 1.8 %copy.37 = f32[512,1024]{1,0:T(8,128)} copy(f32[512,1024]{0,1:T(8,128)S(1)} %get-tuple-element.213) | data formatting | bytes 4194304
  (58 shorter events, 3.1 us)
Async XLA Ops:
  0.6 32.8 %copy-start = (f32[512,512]{1,0:T(8,128)S(1)}, f32[512,512]{1,0:T(8,128)}, u32[]{:S(2)}) copy-start(f32[512,512]{1,0:T(8,128)} %param.11) | copy-start | bytes 3145732
  0.6 9.2 %copy-start.4 = (bf16[56,512]{1,0:T(8,128)(2,1)S(1)}, bf16[56,512]{1,0:T(8,128)(2,1)}, u32[]{:S(2)}) copy-start(bf16[56,512]{1,0:T(8,128)(2,1)} %param.10) | copy-start | bytes 172036
  3.8 23.8 %collective-permute-start = (bf16[56,1024]{1,0:T(8,128)(2,1)}, bf16[56,1024]{1,0:T(8,128)(2,1)}, u32[]{:S(2)}, u32[]{:S(2)}) collective-permute-start(bf16[56,1024]{1,0:T(8,128)(2,1)} %bitcast.57), channel_id=1, source_target_pairs={{0,1},{1,0},{2,3},{3,2},{4,5},{5,4},{6,7},{7,6},{8,9},{9,8},{10,11... | collective-permute-start | bytes 344072 | tf_op jit(solution)/shard_map/ppermute | solution.py:76
  6.6 21.0 %collective-permute-start.1 = (bf16[56,1024]{1,0:T(8,128)(2,1)}, bf16[56,1024]{1,0:T(8,128)(2,1)}, u32[]{:S(2)}, u32[]{:S(2)}) collective-permute-start(bf16[56,1024]{1,0:T(8,128)(2,1)} %bitcast.56), channel_id=1, source_target_pairs={{0,2},{1,3},{2,0},{3,1},{4,6},{5,7},{6,4},{7,5},{8,10},{9,11},{10,... | collective-permute-start | bytes 344072 | tf_op jit(solution)/shard_map/ppermute | solution.py:76
  9.9 17.7 %collective-permute-start.2 = (bf16[56,1024]{1,0:T(8,128)(2,1)}, bf16[56,1024]{1,0:T(8,128)(2,1)}, u32[]{:S(2)}, u32[]{:S(2)}) collective-permute-start(bf16[56,1024]{1,0:T(8,128)(2,1)} %bitcast.55), channel_id=1, source_target_pairs={{0,3},{1,2},{2,1},{3,0},{4,7},{5,6},{6,5},{7,4},{8,11},{9,10},{10,... | collective-permute-start | bytes 344072 | tf_op jit(solution)/shard_map/ppermute | solution.py:76
  23.9 9.5 %copy-start.1 = (f32[512,1024]{0,1:T(8,128)}, f32[512,1024]{0,1:T(8,128)S(1)}, u32[]{:S(2)}) copy-start(f32[512,1024]{0,1:T(8,128)S(1)} %copy.28) | copy-start | bytes 6291460
  31.8 1.7 %copy-start.3 = (f32[512,1024]{0,1:T(8,128)S(1)}, f32[512,1024]{0,1:T(8,128)}, u32[]{:S(2)}) copy-start(f32[512,1024]{0,1:T(8,128)} %copy.29) | copy-start | bytes 6291460
  33.5 5.3 %copy-start.2 = (f32[1024,512]{1,0:T(8,128)}, f32[1024,512]{1,0:T(8,128)S(1)}, u32[]{:S(2)}) copy-start(f32[1024,512]{1,0:T(8,128)S(1)} %fusion.31) | copy-start | bytes 6291460
